TPU v7x, 512 devices: a whole 4x4x16 slice. The times are simulated.
512 devices in a mesh: group: 16 (over x, y), dev: 32 (over z, core).
Axes of the slice: x: 4, y: 4, z: 16, core: 2. Of those that a mesh axis runs over, the one named last changes fastest.
Arguments:
- embeddings: bfloat16 [655360, 768], P(('group', 'dev')), may hold values from -6 to 6
- projection: bfloat16 [256, 768], replicated, may hold values from -0.21875 to 0.21875
- triplets: int32 [3, 1048576], P(None, ('group', 'dev')), may hold values from 0 to 3327, as said below
- cotangent: float32 [1048576], P(('group', 'dev')), may hold values from -24 to 24
- wanted_rows: int32 [8192, 128], P(('group', 'dev')), may hold values from -1 to 1279, as said below
Outputs:
- row_grad: bfloat16 [655360, 768], P(('group', 'dev'))
- weight_grad: float32 [256, 768], replicated
Inputs may be any that keep to these rules, and one draw needn't show every extreme that they name: `wanted_rows`: in each list the live entries come first and are distinct rows of the owning device, the rest are -1; each list holds from 128 // 4 (at least 1) to 128 live entries; all lists of some group of requesters are full, and all lists sent to some group are full. `triplets`: anchors are below 1280; a positive or negative below 1280 is one of the device's own rows, else 1280 + h * 128 + s names a live slot s of the device's list for group h.
All inputs are finite; a program needn't handle non-finite values.
Results may differ from a plain program's by a relative error of at most 0.0058.
Values may be sent and summed in bfloat16 or wider, within the bound.
No kernel may reach another device: no remote copies, remote signals or barrier semaphores. Data moves between devices by JAX's collectives and lax.ppermute only.
A program may use at most 64 MiB of HBM per device.

v0:
```python
import math
import jax
import jax.numpy as jnp
from jax import lax
from jax.sharding import PartitionSpec as P

distance_scale = 0.0625
margin = 1.0
pull_share = 0.5


def triplet_gradients(lookup, triple, cotangent):
    anchor_rows = lookup[triple[0]].astype(jnp.float32)
    positive_rows = lookup[triple[1]].astype(jnp.float32)
    negative_rows = lookup[triple[2]].astype(jnp.float32)
    to_positive = anchor_rows - positive_rows
    to_negative = anchor_rows - negative_rows
    near = distance_scale * jnp.sum(to_positive * to_positive, axis=1)
    far = distance_scale * jnp.sum(to_negative * to_negative, axis=1)
    hinge_gate = jax.nn.sigmoid(margin + near - far)
    pull_factor = 2.0 * distance_scale * cotangent * (1.0 - pull_share + pull_share * hinge_gate)
    push_factor = 2.0 * distance_scale * cotangent * pull_share * hinge_gate
    pull_term = pull_factor[:, None] * to_positive
    push_term = push_factor[:, None] * to_negative
    gradient = jnp.zeros(lookup.shape, jnp.float32)
    gradient = gradient.at[triple[0]].add(pull_term - push_term)
    gradient = gradient.at[triple[1]].add(-pull_term)
    gradient = gradient.at[triple[2]].add(push_term)
    return gradient


def local(embeddings, projection, triplets, cotangent, wanted_rows):
    shard_rows = embeddings.shape[0]
    rank_width = projection.shape[0]
    groups = lax.axis_size("group")
    contract = (((1,), (1,)), ((), ()))
    own_projected = lax.dot_general(
        embeddings, projection, contract, preferred_element_type=jnp.float32
    ).astype(jnp.bfloat16)
    wanted = lax.all_to_all(wanted_rows, "group", split_axis=0, concat_axis=0, tiled=True)
    served_index = jnp.maximum(wanted, 0)
    served = own_projected[served_index]
    fetched = lax.all_to_all(served, "group", split_axis=0, concat_axis=0, tiled=True)
    lookup = jnp.concatenate([own_projected, fetched.reshape(-1, rank_width)], axis=0)
    gradient = triplet_gradients(lookup, triplets, cotangent)
    remote_grad = gradient[shard_rows:].reshape(groups, -1, rank_width).astype(jnp.bfloat16)
    returned = lax.all_to_all(remote_grad, "group", split_axis=0, concat_axis=0, tiled=True)
    row_total = (
        gradient[:shard_rows]
        .at[served_index.reshape(-1)]
        .add(returned.reshape(-1, rank_width).astype(jnp.float32))
    )
    row_rounded = row_total.astype(jnp.bfloat16)
    row_grad = jnp.dot(row_rounded, projection, preferred_element_type=jnp.float32).astype(
        jnp.bfloat16
    )
    partial_value = lax.dot_general(
        row_rounded, embeddings, (((0,), (0,)), ((), ())), preferred_element_type=jnp.float32
    )
    factor = 1.0 / math.sqrt(cotangent.shape[0] * groups * lax.axis_size("dev"))
    weight_total = lax.psum(partial_value, ("group", "dev"))
    return (row_grad, weight_total * factor)


def solution(mesh):
    return jax.shard_map(
        local,
        mesh=mesh,
        in_specs=(
            P(("group", "dev"), None),
            P(),
            P(None, ("group", "dev")),
            P(("group", "dev")),
            P(("group", "dev"), None),
        ),
        out_specs=(P(("group", "dev"), None), P()),
        check_vma=False,
    )
```

profile of v0, /device:TPU:2, one launch (start us, length us, event | category | flops | bytes accessed | tf_op | source)
XLA Modules:
  0.0 648.8 jit_solution(12373123322807966387)
XLA Ops:
  7.2 0.0 copy-start
  7.2 9.3 %all-to-all-start = ((s32[16,1,128]{2,1,0:T(1,128)}), s32[16,1,128]{2,1,0:T(1,128)S(1)}, u32[]{:S(2)}, u32[]{:S(2)}) async-start(s32[16,1,128]{2,1,0:T(1,128)} %bitcast.29), calls=%async_computation | async-start | bytes 16384 | tf_op jit(solution)/shard_map/all_to_all | solution.py:40
  16.5 0.0 copy-done
  16.5 1.7 convolution_convert_fusion.1
  18.2 4.5 all-to-all-done
  22.7 9.1 %gather_fusion = bf16[2048,256]{1,0:T(8,128)(2,1)} fusion(bf16[1280,256]{1,0:T(8,128)(2,1)S(1)} %convolution_convert_fusion.1, s32[2048]{0:T(1024)S(1)} %broadcast_clamp_fusion.3), kind=kCustom, calls=%fused_computation | custom fusion | bytes 2105344 | tf_op jit(solution)/shard_map/gather | solution.py:42
  31.8 0.0 copy-start.1
  31.8 5.7 all-to-all-start.1
  37.4 0.0 copy-done.1
  37.5 12.2 %all-to-all-done.1 = bf16[16,128,256]{2,1,0:T(8,128)(2,1)} async-done(((bf16[16,128,256]{2,1,0:T(8,128)(2,1)}), bf16[16,128,256]{2,1,0:T(8,128)(2,1)}, u32[]{:S(2)}, u32[]{:S(2)}) %all-to-all-start.1) | async-done | bytes 1048608 | tf_op jit(solution)/shard_map/all_to_all | solution.py:43
  49.7 2.5 pad_maximum_fusion
  52.2 8.3 %gather_fusion.1 = bf16[2048,256]{1,0:T(8,128)(2,1)S(1)} fusion(bf16[3328,256]{1,0:T(8,128)(2,1)} %pad_maximum_fusion, s32[2048]{0:T(1024)S(1)} %broadcast_clamp_fusion.2), kind=kCustom, calls=%fused_computation.1 | custom fusion | bytes 2105344 | tf_op jit(solution)/shard_map/gather | solution.py:13
  60.5 10.1 %gather_fusion.3 = bf16[2048,256]{1,0:T(8,128)(2,1)} fusion(bf16[3328,256]{1,0:T(8,128)(2,1)} %pad_maximum_fusion, s32[2048]{0:T(1024)S(1)} %broadcast_clamp_fusion), kind=kCustom, calls=%fused_computation.3 | custom fusion | bytes 2105344 | tf_op jit(solution)/shard_map/gather | solution.py:15
  70.7 10.1 %gather_fusion.2 = bf16[2048,256]{1,0:T(8,128)(2,1)} fusion(bf16[3328,256]{1,0:T(8,128)(2,1)} %pad_maximum_fusion, s32[2048]{0:T(1024)S(1)} %broadcast_clamp_fusion.1), kind=kCustom, calls=%fused_computation.2 | custom fusion | bytes 2105344 | tf_op jit(solution)/shard_map/gather | solution.py:14
  80.8 0.0 copy-start.2
  80.8 2.5 multiply_reduce_fusion.1
  83.3 0.0 copy-done.2
  83.3 15.1 %scatter_custom_fusion = f32[3328,256]{1,0:T(8,128)} fusion(s32[2048]{0:T(1024)S(1)} %bitcast.28, bf16[2048,256]{1,0:T(8,128)(2,1)} %gather_fusion.3, bf16[2048,256]{1,0:T(8,128)(2,1)S(1)} %gather_fusion.1, bf16[2048,256]{1,0:T(8,128)(2,1)} %gather_fusion.2, f32[]{:T(128)} %constant.8.clone.1, f32[2048]{0:T(1024)S(1)} %get-tuple-element.8, ...), kind=kCustom, calls=%fused_computation.17 | custom fusion | flops 4718592 | bytes 6569988 | tf_op jit(solution)/shard_map/scatter-add | solution.py:26
  98.4 16.7 %scatter_custom_fusion.1 = f32[3328,256]{1,0:T(8,128)} fusion(f32[3328,256]{1,0:T(8,128)} %scatter_custom_fusion, s32[2048]{0:T(1024)S(1)} %bitcast.26, bf16[2048,256]{1,0:T(8,128)(2,1)} %gather_fusion.2, bf16[2048,256]{1,0:T(8,128)(2,1)S(1)} %gather_fusion.1, f32[2048]{0:T(1024)S(1)} %get-tuple-element.7), kind=kCustom, calls=%fused_computation.15 | custom fusion | flops 3145728 | bytes 5513216 | tf_op jit(solution)/shard_map/scatter-add | solution.py:27
  115.1 16.6 %scatter_custom_fusion.2 = f32[3328,256]{1,0:T(8,128)} fusion(f32[3328,256]{1,0:T(8,128)} %scatter_custom_fusion.1, s32[2048]{0:T(1024)S(1)} %bitcast.24, bf16[2048,256]{1,0:T(8,128)(2,1)} %gather_fusion.3, bf16[2048,256]{1,0:T(8,128)(2,1)S(1)} %gather_fusion.1, f32[2048]{0:T(1024)S(1)} %get-tuple-element.8), kind=kCustom, calls=%fused_computation.23 | custom fusion | flops 2621440 | bytes 5513216 | tf_op jit(solution)/shard_map/scatter-add | solution.py:28
  131.7 2.7 slice.38
  134.4 6.3 all-to-all-start.2
  140.7 0.0 all-reduce.2.cloned.1.call-start
  140.8 1.4 slice.32
  142.2 9.6 %all-to-all-done.2 = bf16[16,128,256]{2,1,0:T(8,128)(2,1)} async-done(((bf16[16,128,256]{2,1,0:T(8,128)(2,1)}), bf16[16,128,256]{2,1,0:T(8,128)(2,1)}, u32[]{:S(2)}, u32[]{:S(2)}) %all-to-all-start.2) | async-done | bytes 1048608 | tf_op jit(solution)/shard_map/all_to_all | solution.py:47
  151.7 13.6 %scatter_custom_fusion.3 = f32[1280,256]{1,0:T(8,128)S(1)} fusion(f32[1280,256]{1,0:T(8,128)S(1)} %slice.32, s32[2048]{0:T(1024)S(1)} %bitcast.22, bf16[2048,256]{1,0:T(8,128)(2,1)} %bitcast.12), kind=kCustom, calls=%fused_computation.13 | custom fusion | flops 1048576 | bytes 2359296 | tf_op jit(solution)/shard_map/scatter-add | solution.py:51
  165.3 1.6 fusion.18
  166.9 0.0 all-reduce.2.cloned.1.call-update
  166.9 2.9 convolution_convert_fusion
  169.9 470.0 %all-reduce.2.cloned.1.call-done = f32[256,768]{1,0:T(8,128)} async-done(((f32[256,768]{1,0:T(8,128)}), f32[256,768]{1,0:T(8,128)}) %all-reduce.2.cloned.1.call-update) | async-done | bytes 786448 | tf_op jit(solution)/shard_map/psum | solution.py:61
  639.9 2.1 broadcast_multiply_fusion
  (7 shorter events, 0.1 us)
Async XLA Ops:
  7.2 9.3 %copy-start = (bf16[1280,768]{1,0:T(8,128)(2,1)S(1)}, bf16[1280,768]{1,0:T(8,128)(2,1)}, u32[]{:S(2)}) copy-start(bf16[1280,768]{1,0:T(8,128)(2,1)} %param.5) | copy-start | bytes 5898244
  7.2 15.5 %all-to-all-start = ((s32[16,1,128]{2,1,0:T(1,128)}), s32[16,1,128]{2,1,0:T(1,128)S(1)}, u32[]{:S(2)}, u32[]{:S(2)}) async-start(s32[16,1,128]{2,1,0:T(1,128)} %bitcast.29), calls=%async_computation | async-start | bytes 16384 | tf_op jit(solution)/shard_map/all_to_all | solution.py:40
  31.8 5.7 copy-start.1
  31.8 17.9 %all-to-all-start.1 = ((bf16[16,128,256]{2,1,0:T(8,128)(2,1)}), bf16[16,128,256]{2,1,0:T(8,128)(2,1)}, u32[]{:S(2)}, u32[]{:S(2)}) async-start(bf16[16,128,256]{2,1,0:T(8,128)(2,1)} %bitcast.20), calls=%async_computation.1 | async-start | bytes 2097152 | tf_op jit(solution)/shard_map/all_to_all | solution.py:43
  80.8 2.5 copy-start.2
  134.4 17.3 %all-to-all-start.2 = ((bf16[16,128,256]{2,1,0:T(8,128)(2,1)}), bf16[16,128,256]{2,1,0:T(8,128)(2,1)}, u32[]{:S(2)}, u32[]{:S(2)}) async-start(bf16[16,128,256]{2,1,0:T(8,128)(2,1)} %bitcast.10), calls=%async_computation.2 | async-start | bytes 2097152 | tf_op jit(solution)/shard_map/all_to_all | solution.py:47
  140.7 499.1 %all-reduce.2.cloned.1.call-start = ((), (), s32[]{:S(2)}) async-start(), calls=%async_computation.3 | async-start | bytes 1572864 | tf_op jit(solution)/shard_map/psum | solution.py:61
Sparse Core Ops, SparseCore 0:
  167.0 472.7 all-reduce.1
where the time goes:
time: 650 us; the launch traced here: 649 us
  waiting for transfers between devices  496 us (76%)
  other arithmetic  69.2 us (11%)
  local copies, waits for them, and re-layouts  41.7 us (6%)
  starting transfers between devices  21.3 us (3%)
  between operations  14.1 us (2%)
    psum x1, waiting for transfers between devices, local(): weight_total = lax.psum(partial_value, ('group', 'dev'))  470 us
    scatter-add x1, other arithmetic, triplet_gradients(): gradient = gradient.at[triple[1]].add(-pull_term)  16.7 us
    scatter-add x1, other arithmetic, triplet_gradients(): gradient = gradient.at[triple[2]].add(push_term)  16.6 us
    scatter-add x1, other arithmetic, triplet_gradients(): gradient = gradient.at[triple[0]].add(pull_term - push_term)  15.1 us
    scatter-add x1, other arithmetic, local(): row_total = gradient[:shard_rows].at[served_index.reshape(-1)].add(return...  13.6 us
  transfers between devices with their start and end apart: 4, of which 4 were waited for; matrix products, arithmetic and copies ran while one was open for 1% of the time, Pallas kernels for 0%

commit v1 on v0

--- a/solution.py
+++ b/solution.py
@@ -58,7 +58,7 @@
         row_rounded, embeddings, (((0,), (0,)), ((), ())), preferred_element_type=jnp.float32
     )
     factor = 1.0 / math.sqrt(cotangent.shape[0] * groups * lax.axis_size("dev"))
-    weight_total = lax.psum(partial_value, ("group", "dev"))
+    weight_total = lax.psum(lax.psum(partial_value, "group"), "dev")
     return (row_grad, weight_total * factor)
 
 

time: 650 us -> 511 us (0.79)
  the two profiles are of different devices: /device:TPU:2 before, /device:TPU:1 now
where the time goes in v1:
time: 511 us; the launch traced here: 510 us
  waiting for transfers between devices  362 us (71%)
  other arithmetic  69 us (14%)
  local copies, waits for them, and re-layouts  41.7 us (8%)
  starting transfers between devices  16.6 us (3%)
  between operations  14.2 us (3%)
  matrix products  6.24 us (1%)
    psum x2, waiting for transfers between devices, local(): weight_total = lax.psum(lax.psum(partial_value, 'group'), 'dev')  335 us
    scatter-add x1, other arithmetic, triplet_gradients(): gradient = gradient.at[triple[1]].add(-pull_term)  16.7 us
    scatter-add x1, other arithmetic, triplet_gradients(): gradient = gradient.at[triple[2]].add(push_term)  16.6 us
    scatter-add x1, other arithmetic, triplet_gradients(): gradient = gradient.at[triple[0]].add(pull_term - push_term)  15.1 us
    scatter-add x1, other arithmetic, local(): row_total = gradient[:shard_rows].at[served_index.reshape(-1)].add(return...  13.4 us
    all_to_all x1, waiting for transfers between devices, local(): lax.all_to_all(served, 'group', split_axis=0, concat_axis=0, tiled=True)  12.3 us
    all_to_all x1, waiting for transfers between devices, local(): lax.all_to_all(remote_grad, 'group', split_axis=0, concat_axis=0, tiled=T...  10.4 us
  transfers between devices with their start and end apart: 5, of which 5 were waited for; matrix products, arithmetic and copies ran while one was open for 1% of the time, Pallas kernels for 0%

profile of v1, /device:TPU:1, one launch (start us, length us, event | category | flops | bytes accessed | tf_op | source)
XLA Modules:
  0.0 509.9 jit_solution(5046727615045118211)
XLA Ops:
  7.2 0.0 copy-start
  7.2 7.7 %all-to-all-start = ((s32[16,1,128]{2,1,0:T(1,128)}), s32[16,1,128]{2,1,0:T(1,128)S(1)}, u32[]{:S(2)}, u32[]{:S(2)}) async-start(s32[16,1,128]{2,1,0:T(1,128)} %bitcast.29), calls=%async_computation | async-start | bytes 16384 | tf_op jit(solution)/shard_map/all_to_all | solution.py:40
  14.9 0.0 copy-done
  14.9 1.7 convolution_convert_fusion.1
  16.6 4.6 all-to-all-done
  21.3 9.1 %gather_fusion = bf16[2048,256]{1,0:T(8,128)(2,1)} fusion(bf16[1280,256]{1,0:T(8,128)(2,1)S(1)} %convolution_convert_fusion.1, s32[2048]{0:T(1024)S(1)} %broadcast_clamp_fusion.3), kind=kCustom, calls=%fused_computation | custom fusion | bytes 2105344 | tf_op jit(solution)/shard_map/gather | solution.py:42
  30.3 0.0 copy-start.1
  30.3 4.5 all-to-all-start.1
  34.8 0.0 copy-done.1
  34.9 12.3 %all-to-all-done.1 = bf16[16,128,256]{2,1,0:T(8,128)(2,1)} async-done(((bf16[16,128,256]{2,1,0:T(8,128)(2,1)}), bf16[16,128,256]{2,1,0:T(8,128)(2,1)}, u32[]{:S(2)}, u32[]{:S(2)}) %all-to-all-start.1) | async-done | bytes 1048608 | tf_op jit(solution)/shard_map/all_to_all | solution.py:43
  47.2 2.5 pad_maximum_fusion
  49.7 8.3 %gather_fusion.1 = bf16[2048,256]{1,0:T(8,128)(2,1)S(1)} fusion(bf16[3328,256]{1,0:T(8,128)(2,1)} %pad_maximum_fusion, s32[2048]{0:T(1024)S(1)} %broadcast_clamp_fusion.2), kind=kCustom, calls=%fused_computation.1 | custom fusion | bytes 2105344 | tf_op jit(solution)/shard_map/gather | solution.py:13
  58.0 10.1 %gather_fusion.3 = bf16[2048,256]{1,0:T(8,128)(2,1)} fusion(bf16[3328,256]{1,0:T(8,128)(2,1)} %pad_maximum_fusion, s32[2048]{0:T(1024)S(1)} %broadcast_clamp_fusion), kind=kCustom, calls=%fused_computation.3 | custom fusion | bytes 2105344 | tf_op jit(solution)/shard_map/gather | solution.py:15
  68.1 10.1 %gather_fusion.2 = bf16[2048,256]{1,0:T(8,128)(2,1)} fusion(bf16[3328,256]{1,0:T(8,128)(2,1)} %pad_maximum_fusion, s32[2048]{0:T(1024)S(1)} %broadcast_clamp_fusion.1), kind=kCustom, calls=%fused_computation.2 | custom fusion | bytes 2105344 | tf_op jit(solution)/shard_map/gather | solution.py:14
  78.2 0.0 copy-start.2
  78.2 2.5 multiply_reduce_fusion.1
  80.7 0.0 copy-done.2
  80.8 15.1 %scatter_custom_fusion = f32[3328,256]{1,0:T(8,128)} fusion(s32[2048]{0:T(1024)S(1)} %bitcast.28, bf16[2048,256]{1,0:T(8,128)(2,1)} %gather_fusion.3, bf16[2048,256]{1,0:T(8,128)(2,1)S(1)} %gather_fusion.1, bf16[2048,256]{1,0:T(8,128)(2,1)} %gather_fusion.2, f32[]{:T(128)} %constant.8.clone.1, f32[2048]{0:T(1024)S(1)} %get-tuple-element.8, ...), kind=kCustom, calls=%fused_computation.17 | custom fusion | flops 4718592 | bytes 6569988 | tf_op jit(solution)/shard_map/scatter-add | solution.py:26
  95.9 16.7 %scatter_custom_fusion.1 = f32[3328,256]{1,0:T(8,128)} fusion(f32[3328,256]{1,0:T(8,128)} %scatter_custom_fusion, s32[2048]{0:T(1024)S(1)} %bitcast.26, bf16[2048,256]{1,0:T(8,128)(2,1)} %gather_fusion.2, bf16[2048,256]{1,0:T(8,128)(2,1)S(1)} %gather_fusion.1, f32[2048]{0:T(1024)S(1)} %get-tuple-element.7), kind=kCustom, calls=%fused_computation.15 | custom fusion | flops 3145728 | bytes 5513216 | tf_op jit(solution)/shard_map/scatter-add | solution.py:27
  112.6 16.6 %scatter_custom_fusion.2 = f32[3328,256]{1,0:T(8,128)} fusion(f32[3328,256]{1,0:T(8,128)} %scatter_custom_fusion.1, s32[2048]{0:T(1024)S(1)} %bitcast.24, bf16[2048,256]{1,0:T(8,128)(2,1)} %gather_fusion.3, bf16[2048,256]{1,0:T(8,128)(2,1)S(1)} %gather_fusion.1, f32[2048]{0:T(1024)S(1)} %get-tuple-element.8), kind=kCustom, calls=%fused_computation.23 | custom fusion | flops 2621440 | bytes 5513216 | tf_op jit(solution)/shard_map/scatter-add | solution.py:28
  129.2 2.7 slice.38
  131.9 4.4 all-to-all-start.2
  136.2 0.0 all-reduce.3.cloned.1.call-start
  136.3 1.4 slice.32
  137.7 10.4 %all-to-all-done.2 = bf16[16,128,256]{2,1,0:T(8,128)(2,1)} async-done(((bf16[16,128,256]{2,1,0:T(8,128)(2,1)}), bf16[16,128,256]{2,1,0:T(8,128)(2,1)}, u32[]{:S(2)}, u32[]{:S(2)}) %all-to-all-start.2) | async-done | bytes 1048608 | tf_op jit(solution)/shard_map/all_to_all | solution.py:47
  148.1 13.4 %scatter_custom_fusion.3 = f32[1280,256]{1,0:T(8,128)S(1)} fusion(f32[1280,256]{1,0:T(8,128)S(1)} %slice.32, s32[2048]{0:T(1024)S(1)} %bitcast.22, bf16[2048,256]{1,0:T(8,128)(2,1)} %bitcast.12), kind=kCustom, calls=%fused_computation.13 | custom fusion | flops 1048576 | bytes 2359296 | tf_op jit(solution)/shard_map/scatter-add | solution.py:51
  161.6 1.6 fusion.18
  163.2 0.0 all-reduce.3.cloned.1.call-update
  163.2 0.0 all-reduce.5.cloned.1.call-start
  163.2 124.8 %all-reduce.3.cloned.1.call-done = f32[256,768]{1,0:T(8,128)} async-done(((f32[256,768]{1,0:T(8,128)}), f32[256,768]{1,0:T(8,128)}) %all-reduce.3.cloned.1.call-update) | async-done | bytes 786448 | tf_op jit(solution)/shard_map/psum | solution.py:61
  288.0 0.0 all-reduce.5.cloned.1.call-update
  288.1 2.9 convolution_convert_fusion
  291.0 210.0 %all-reduce.5.cloned.1.call-done = f32[256,768]{1,0:T(8,128)} async-done(((f32[256,768]{1,0:T(8,128)}), f32[256,768]{1,0:T(8,128)}) %all-reduce.5.cloned.1.call-update) | async-done | bytes 786448 | tf_op jit(solution)/shard_map/psum | solution.py:61
  501.0 2.1 broadcast_multiply_fusion
  (7 shorter events, 0.1 us)
Async XLA Ops:
  7.2 7.8 %copy-start = (bf16[1280,768]{1,0:T(8,128)(2,1)S(1)}, bf16[1280,768]{1,0:T(8,128)(2,1)}, u32[]{:S(2)}) copy-start(bf16[1280,768]{1,0:T(8,128)(2,1)} %param.5) | copy-start | bytes 5898244
  7.2 14.1 %all-to-all-start = ((s32[16,1,128]{2,1,0:T(1,128)}), s32[16,1,128]{2,1,0:T(1,128)S(1)}, u32[]{:S(2)}, u32[]{:S(2)}) async-start(s32[16,1,128]{2,1,0:T(1,128)} %bitcast.29), calls=%async_computation | async-start | bytes 16384 | tf_op jit(solution)/shard_map/all_to_all | solution.py:40
  30.3 4.5 copy-start.1
  30.3 16.8 %all-to-all-start.1 = ((bf16[16,128,256]{2,1,0:T(8,128)(2,1)}), bf16[16,128,256]{2,1,0:T(8,128)(2,1)}, u32[]{:S(2)}, u32[]{:S(2)}) async-start(bf16[16,128,256]{2,1,0:T(8,128)(2,1)} %bitcast.20), calls=%async_computation.1 | async-start | bytes 2097152 | tf_op jit(solution)/shard_map/all_to_all | solution.py:43
  78.2 2.5 copy-start.2
  131.9 16.3 %all-to-all-start.2 = ((bf16[16,128,256]{2,1,0:T(8,128)(2,1)}), bf16[16,128,256]{2,1,0:T(8,128)(2,1)}, u32[]{:S(2)}, u32[]{:S(2)}) async-start(bf16[16,128,256]{2,1,0:T(8,128)(2,1)} %bitcast.10), calls=%async_computation.2 | async-start | bytes 2097152 | tf_op jit(solution)/shard_map/all_to_all | solution.py:47
  136.2 151.8 %all-reduce.3.cloned.1.call-start = ((), (), s32[]{:S(2)}) async-start(), calls=%async_computation.3 | async-start | bytes 1572864 | tf_op jit(solution)/shard_map/psum | solution.py:61
  163.2 337.8 %all-reduce.5.cloned.1.call-start = ((), (), s32[]{:S(2)}) async-start(), calls=%async_computation.4 | async-start | bytes 1572864 | tf_op jit(solution)/shard_map/psum | solution.py:61
Sparse Core Ops, SparseCore 0:
  163.3 124.6 all-reduce.2
  290.5 210.4 all-reduce.4
